TPU v7x, 256 devices: a whole 4x4x8 slice. The times are simulated.
256 devices in a mesh: depth: 16 (over z, core), slab: 16 (over y, x).
Axes of the slice: x: 4, y: 4, z: 8, core: 2. Of those that a mesh axis runs over, the one named last changes fastest.
Arguments:
- state: float32 [16, 2, 2048, 2048], P('depth', None, 'slab'), may hold values from -6 to 6
- fresh: float32 [2, 2, 2048, 2048], P(None, None, 'slab'), may hold values from -6 to 6
- operators: float32 [4, 2, 2, 384, 128], replicated
- band: int32 [16], P('depth'), may hold values from 0 to 1
- freq_sched: int32 [18], replicated, may hold values from 0 to 3
Outputs:
- state_out: float32 [16, 2, 2048, 2048], P('depth', None, 'slab')
- image: float32 [16, 2048], P('depth', 'slab')
All inputs are finite; a program needn't handle non-finite values.
Results may differ from a plain program's by a relative error of at most 0.00011.
Values sent between devices are 32-bit elements; how exact they have to be, the bound alone decides.
A program may use at most 128 MiB of HBM per device.

v0:
```python
import functools

import jax
import jax.numpy as jnp
from jax import lax
from jax.experimental import pallas as pl
from jax.experimental.pallas import tpu as pltpu
from jax.sharding import PartitionSpec as P

MESH = pl.DeviceIdType.MESH
F32, BF16 = jnp.float32, jnp.bfloat16
W = 128
ND = 16
NS = 16
NP = NS // 2


def dot(a, b):
    return jnp.dot(a, b, preferred_element_type=F32)


def split(x):
    hi = x.astype(BF16)
    return hi, (x - hi.astype(F32)).astype(BF16)


def diagonal(square):
    rows = lax.broadcasted_iota(jnp.int32, (W, W), 0)
    cols = lax.broadcasted_iota(jnp.int32, (W, W), 1)
    return jnp.sum(jnp.where(rows == cols, square, 0.0), axis=0, keepdims=True)


def lanes(block, count=1):
    return pl.ds(pl.multiple_of(block * W, W), count * W)


def kernel(
    freq, band, state, fresh, operators, out, image,
    x, ops, a_hi, a_lo, b0_hi, b0_lo, b1_hi, b1_lo, wr_hi, wr_lo, ws0, ws1,
    send1, recv1, send2, recv2, obuf, tiles, y, i0, i1, r0, r1,
    in_sem, out_sem, s1_sem, r1_sem, s2_sem, r2_sem, sb_sem, rb_sem, sy_sem, ry_sem, si_sem, ri_sem,
):
    d, me = lax.axis_index("depth"), lax.axis_index("slab")
    c = lax.rem(d, 2)
    pair = me // 2
    odd = lax.rem(me, 2)
    wrap = lambda k: lax.rem(k + 2 * ND, ND)
    before, after = wrap(d - 2), wrap(d + 2)
    there1 = wrap(d + 2 * c)
    there2 = wrap(d + 2 * (1 - c))
    last = d == ND - 1
    relayed = d == 1
    at = lambda depth, slab: {"depth": depth, "slab": slab}

    ops_in = pltpu.make_async_copy(operators, ops, in_sem.at[0])
    x_in = [
        pltpu.make_async_copy(state.at[0, :, :, q * 512 : q * 512 + 512], x.at[:, :, q * 512 : q * 512 + 512], in_sem.at[1 + q])
        for q in range(4)
    ]
    ops_in.start()
    for copy in x_in:
        copy.start()

    barrier = pltpu.get_barrier_semaphore()
    signal = lambda depth, slab: pl.semaphore_signal(barrier, inc=1, device_id=at(depth, slab), device_id_type=MESH)

    @pl.loop(0, NS)
    def _(j):
        signal(before, j)

        @pl.when(j != me)
        def _():
            signal(d, j)

    signal(wrap(d - 1), me)
    signal(wrap(d + 1), me)
    signal(after, me)

    tiles[3] = jnp.full((8, W), band[0], jnp.int32)

    def operator(k, tick, tile):
        f = freq[2 - tick + k]
        pick = tiles[tile][0:1, :] > 0

        def part(component, block):
            rows = slice(block * W, block * W + W)
            return jnp.where(pick, ops[f, 1, component, rows, :], ops[f, 0, component, rows, :])

        return part

    def build_r(part):
        for block in range(3):
            re, im = part(0, block), part(1, block)
            base = block * 2 * W
            for row, left, right in ((0, re, im), (W, -im, re)):
                for col, value in ((0, left), (W, right)):
                    hi, lo = split(value)
                    wr_hi[base + row : base + row + W, col : col + W] = hi
                    wr_lo[base + row : base + row + W, col : col + W] = lo

    def build_s(part, ws):
        for block in range(3):
            re, im = part(0, block).T, part(1, block).T
            base = block * 2 * W
            for col, top, bottom in ((0, re, im), (W, -im, re)):
                for row, value in ((0, top), (W, bottom)):
                    hi, lo = split(value)
                    ws[row : row + W, base + col : base + col + W] = hi
                    ws[2 * W + row : 2 * W + row + W, base + col : base + col + W] = lo

    for ref in (a_hi, a_lo):
        ref[:, 0 : 2 * W] = jnp.zeros((W, 2 * W), BF16)
        ref[:, (NS + 1) * 2 * W :] = jnp.zeros((W, 2 * W), BF16)
    for ref in (b0_hi, b0_lo, b1_hi, b1_lo):
        ref[0 : 2 * W, 0:W] = jnp.zeros((2 * W, W), BF16)
        ref[NS * 2 * W :, W : 2 * W] = jnp.zeros((2 * W, W), BF16)

    ops_in.wait()
    build_r(operator(d, 0, 3))

    def put_a(block, re, im):
        for offset, value in ((0, re), (1, im)):
            hi, lo = split(value)
            where = lanes((block + 1) * 2 + offset)
            a_hi[:, where] = hi
            a_lo[:, where] = lo

    for q in range(4):
        x_in[q].wait()

        @pl.loop(4 * q, 4 * q + 4)
        def _(b):
            put_a(b, x[0, :, lanes(b)], x[1, :, lanes(b)])

    def along_receivers(p):
        first, second = lanes(4 * p, 6), lanes(4 * p + 2, 6)
        hi = jnp.concatenate([a_hi[:, first], a_hi[:, second]], axis=0)
        lo = jnp.concatenate([a_lo[:, first], a_lo[:, second]], axis=0)
        both = dot(jnp.concatenate([hi, lo], axis=0), wr_hi[...])
        return both[: 2 * W] + both[2 * W :] + dot(hi, wr_lo[...])

    def along_shots(p, ws, b_hi, b_lo):
        rows = pl.ds(pl.multiple_of(p * 4 * W, 4 * W), 6 * W)
        both = dot(ws[...], b_hi[rows, :])
        return both[: 2 * W] + both[2 * W :] + dot(ws[: 2 * W, :], b_lo[rows, :])

    pl.semaphore_wait(barrier, 2 * NS - 1 + 3)

    band_to = (after, wrap(d + 1), wrap(d - 1))
    band_copies = [
        pltpu.make_async_remote_copy(
            src_ref=tiles.at[3], dst_ref=tiles.at[n], send_sem=sb_sem.at[n], recv_sem=rb_sem.at[n],
            device_id=at(band_to[n], me), device_id_type=MESH,
        )
        for n in range(3)
    ]
    for copy in band_copies:
        copy.start()

    def copy1(t):
        return pltpu.make_async_remote_copy(
            src_ref=send1.at[t], dst_ref=recv1.at[me], send_sem=s1_sem.at[t], recv_sem=r1_sem.at[me],
            device_id=at(there1, t), device_id_type=MESH,
        )

    def arrival1(j):
        return pltpu.make_async_remote_copy(
            src_ref=send1.at[j], dst_ref=recv1.at[j], send_sem=s1_sem.at[j], recv_sem=r1_sem.at[j],
            device_id=at(there1, j), device_id_type=MESH,
        )

    def start1(t):
        stays = (c == 0) & (t == me)

        @pl.when(stays)
        def _():
            pltpu.make_async_copy(send1.at[t], recv1.at[me], r1_sem.at[me]).start()

        @pl.when(jnp.logical_not(stays | last))
        def _():
            copy1(t).start()

        @pl.when(last)
        def _():
            pltpu.make_async_remote_copy(
                src_ref=fresh.at[0, :, :, lanes(t)], dst_ref=recv1.at[me], send_sem=s1_sem.at[t], recv_sem=r1_sem.at[me],
                device_id=at(there1, t), device_id_type=MESH,
            ).start()

    def copy2(t):
        return pltpu.make_async_remote_copy(
            src_ref=send2.at[t], dst_ref=recv2.at[me], send_sem=s2_sem.at[t], recv_sem=r2_sem.at[me],
            device_id=at(there2, t), device_id_type=MESH,
        )

    def arrival2(j):
        return pltpu.make_async_remote_copy(
            src_ref=send2.at[j], dst_ref=recv2.at[j], send_sem=s2_sem.at[j], recv_sem=r2_sem.at[j],
            device_id=at(there2, j), device_id_type=MESH,
        )

    def start2(t):
        stays = (c == 1) & (t == me)

        @pl.when(stays)
        def _():
            pltpu.make_async_copy(send2.at[t], recv2.at[me], r2_sem.at[me]).start()

        @pl.when(jnp.logical_not(stays))
        def _():
            copy2(t).start()

    @pl.loop(0, NP)
    def _(i):
        p = lax.rem(pair - i + NP, NP)
        done = along_receivers(p)
        for n in range(2):
            for part in range(2):
                send1[2 * p + n, part] = done[n * W : n * W + W, part * W : part * W + W]
        start1(2 * p)
        start1(2 * p + 1)

    y_right = pltpu.make_async_remote_copy(
        src_ref=send1.at[jnp.minimum(me + 1, NS - 1)], dst_ref=y.at[0], send_sem=sy_sem.at[0], recv_sem=ry_sem.at[0],
        device_id=at(d, jnp.minimum(me + 1, NS - 1)), device_id_type=MESH,
    )
    y_left = pltpu.make_async_remote_copy(
        src_ref=send1.at[jnp.maximum(me - 1, 0)], dst_ref=y.at[1], send_sem=sy_sem.at[1], recv_sem=ry_sem.at[1],
        device_id=at(d, jnp.maximum(me - 1, 0)), device_id_type=MESH,
    )
    has_right, has_left = last & (me < NS - 1), last & (me > 0)
    pl.when(has_right)(y_right.start)
    pl.when(has_left)(y_left.start)

    for copy in band_copies:
        copy.wait_recv()
    swath = wrap(d - 2 * c)
    build_s(operator(swath, 0, 3 - 3 * c), ws0)
    build_s(operator(wrap(swath + 1), 1, 2 - c), ws1)
    build_r(operator(wrap(d - 1), 1, 1))

    def put_b(b_hi, b_lo, block, value):
        hi, lo = split(value)
        down = pl.ds(pl.multiple_of((block + 1) * 2 * W, 2 * W), 2 * W)
        here = pl.ds(pl.multiple_of(block * 2 * W, 2 * W), 2 * W)
        b_hi[down, 0:W] = hi
        b_hi[here, W : 2 * W] = hi
        b_lo[down, 0:W] = lo
        b_lo[here, W : 2 * W] = lo

    @pl.loop(0, NP + 4)
    def _(i):
        @pl.when(i < NP)
        def _():
            p = lax.rem(pair + i, NP)
            for n in range(2):
                arrival1(2 * p + n).wait_recv()

            def put(b_hi, b_lo):
                for n in range(2):
                    put_b(b_hi, b_lo, 2 * p + n, recv1[2 * p + n].reshape(2 * W, W))

            @pl.when(relayed)
            def _():
                put(b1_hi, b1_lo)

            @pl.when(jnp.logical_not(relayed))
            def _():
                put(b0_hi, b0_lo)

        @pl.when((i >= 2) & (i < NP + 2) & jnp.logical_not(relayed))
        def _():
            p = lax.rem(pair + 1 + i - 2, NP)
            done = along_shots(p, ws0, b0_hi, b0_lo)
            put_b(b1_hi, b1_lo, 2 * p, done[:, :W])
            put_b(b1_hi, b1_lo, 2 * p + 1, done[:, W:])

            @pl.when(p == pair)
            def _():
                square = jnp.where(odd == 0, done[:W, :W], done[:W, W:])
                i0[...] = jnp.broadcast_to(diagonal(square), (8, W))

        @pl.when(i >= 4)
        def _():
            p = lax.rem(pair + 2 + i - 4, NP)
            done = along_shots(p, ws1, b1_hi, b1_lo)
            for n in range(2):
                send2[2 * p + n] = done[:, n * W : n * W + W].reshape(2, W, W)
            start2(2 * p)
            start2(2 * p + 1)

    image0 = pltpu.make_async_remote_copy(
        src_ref=i0, dst_ref=r0, send_sem=si_sem.at[0], recv_sem=ri_sem.at[0], device_id=at(before, me), device_id_type=MESH
    )
    sends_image0 = (c == 1) & jnp.logical_not(relayed)
    pl.when(sends_image0)(image0.start)

    @pl.when(last)
    def _():
        @pl.when(me > 0)
        def _():
            y_right.wait_recv()

        @pl.when(me < NS - 1)
        def _():
            y_left.wait_recv()

        @pl.when(me == 0)
        def _():
            y[0] = jnp.zeros((2, W, W), F32)

        @pl.when(me == NS - 1)
        def _():
            y[1] = jnp.zeros((2, W, W), F32)

        part = operator(d, 0, 3)
        total = jnp.zeros((1, W), F32)
        for block, value in ((0, y[0]), (1, send1[me]), (2, y[1])):
            total += jnp.sum(value[0] * part(0, block) - value[1] * part(1, block), axis=0, keepdims=True)
        r0[...] = jnp.broadcast_to(total, (8, W))

    image1 = pltpu.make_async_remote_copy(
        src_ref=i1, dst_ref=r1, send_sem=si_sem.at[1], recv_sem=ri_sem.at[1], device_id=at(wrap(d - 1), me), device_id_type=MESH
    )

    def out_copy(p):
        return pltpu.make_async_copy(obuf.at[:, :, lanes(2 * p, 2)], out.at[0, :, :, lanes(2 * p, 2)], out_sem.at[p])

    @pl.loop(0, NP + 2)
    def _(i):
        @pl.when(i < NP)
        def _():
            p = lax.rem(pair - 2 - i + 2 * NP, NP)
            for n in range(2):
                arrival2(2 * p + n).wait_recv()
                put_a(2 * p + n, recv2[2 * p + n, 0], recv2[2 * p + n, 1])

        @pl.when(i >= 2)
        def _():
            p = lax.rem(pair - 3 - (i - 2) + 2 * NP, NP)
            done = along_receivers(p)
            for part in range(2):
                obuf[part, :, lanes(2 * p)] = done[:W, part * W : part * W + W]
                obuf[part, :, lanes(2 * p + 1)] = done[W:, part * W : part * W + W]
            out_copy(p).start()

            @pl.when(p == pair)
            def _():
                square = jnp.where(odd == 0, done[:W, :W], done[W:, :W])
                i1[...] = jnp.broadcast_to(diagonal(square), (8, W))
                image1.start()

    for copy in band_copies:
        copy.wait_send()
    pl.when(has_right)(y_right.wait_send)
    pl.when(has_left)(y_left.wait_send)

    @pl.loop(0, NS)
    def _(t):
        @pl.when(jnp.logical_not((c == 0) & (t == me)))
        def _():
            copy1(t).wait_send()

        @pl.when(jnp.logical_not((c == 1) & (t == me)))
        def _():
            copy2(t).wait_send()

    pl.when(sends_image0)(image0.wait_send)
    image1.wait_send()
    image1.wait_recv()
    pl.when((c == 1) & jnp.logical_not(last))(image0.wait_recv)

    @pl.when(c == 0)
    def _():
        image[...] = i0[0:1, :] + r1[0:1, :]

    @pl.when(c == 1)
    def _():
        image[...] = r0[0:1, :] + r1[0:1, :]

    @pl.loop(0, NP)
    def _(p):
        out_copy(p).wait()


def body(state, fresh, operators, band, freq_sched):
    any_space = pl.BlockSpec(memory_space=pl.ANY)
    smem = pl.BlockSpec(memory_space=pltpu.SMEM)
    dma, vmem = pltpu.SemaphoreType.DMA, pltpu.VMEM
    rows = state.shape[2]
    out, image = pl.pallas_call(
        kernel,
        name="relay",
        out_shape=(jax.ShapeDtypeStruct(state.shape, F32), jax.ShapeDtypeStruct((1, rows), F32)),
        in_specs=[smem, smem, any_space, any_space, any_space],
        out_specs=(any_space, pl.BlockSpec(memory_space=pltpu.VMEM)),
        scratch_shapes=[
            vmem(state.shape[1:], F32),
            vmem(operators.shape, F32),
            vmem((W, (NS + 2) * 2 * W), BF16),
            vmem((W, (NS + 2) * 2 * W), BF16),
            vmem(((NS + 1) * 2 * W, 2 * W), BF16),
            vmem(((NS + 1) * 2 * W, 2 * W), BF16),
            vmem(((NS + 1) * 2 * W, 2 * W), BF16),
            vmem(((NS + 1) * 2 * W, 2 * W), BF16),
            vmem((6 * W, 2 * W), BF16),
            vmem((6 * W, 2 * W), BF16),
            vmem((4 * W, 6 * W), BF16),
            vmem((4 * W, 6 * W), BF16),
            vmem((NS, 2, W, W), F32),
            vmem((NS, 2, W, W), F32),
            vmem((NS, 2, W, W), F32),
            vmem((NS, 2, W, W), F32),
            vmem(state.shape[1:], F32),
            vmem((4, 8, W), jnp.int32),
            vmem((2, 2, W, W), F32),
            vmem((8, W), F32),
            vmem((8, W), F32),
            vmem((8, W), F32),
            vmem((8, W), F32),
            dma((5,)),
            dma((NP,)),
            dma((NS,)),
            dma((NS,)),
            dma((NS,)),
            dma((NS,)),
            dma((3,)),
            dma((3,)),
            dma((2,)),
            dma((2,)),
            dma((2,)),
            dma((2,)),
        ],
        compiler_params=pltpu.CompilerParams(collective_id=0, has_side_effects=True, vmem_limit_bytes=56 << 20),
    )(freq_sched, band, state, fresh, operators)
    entered = lax.axis_index("depth") == 0
    return jnp.where(entered, fresh[1][None], out), image


def solution(mesh):
    return jax.shard_map(
        body,
        mesh=mesh,
        in_specs=(P("depth", None, "slab", None), P(None, None, "slab", None), P(), P("depth"), P()),
        out_specs=(P("depth", None, "slab", None), P("depth", "slab")),
        check_vma=False,
    )
```

profile of v0, /device:TPU:137, one launch (start us, length us, event | category | flops | bytes accessed | tf_op | source)
XLA Modules:
  0.0 89.3 jit_solution(9469361673550430635)
XLA Ops:
  1.3 0.0 copy-start
  1.3 84.2 %relay.1 = (f32[1,2,128,2048]{3,2,1,0:T(8,128)}, f32[1,128]{1,0:T(1,128)}) custom-call(s32[18]{0:T(128)} %freq.1, s32[1]{0:T(128)S(6)} %copy.8.band, f32[1,2,128,2048]{3,2,1,0:T(8,128)} %state.1, f32[2,2,128,2048]{3,2,1,0:T(8,128)} %fresh.1, f32[4,2,2,384,128]{4,3,2,1,0:T(8,128)} %operators.1), custom_call_target="tpu_custom_call" | custom-call | tf_op jit(solution)/shard_map/relay/pallas_call | solution.py:391
  85.5 0.0 copy-done
  85.5 0.0 copy-start.1
  85.5 3.3 %slice_select_fusion = f32[1,2,128,2048]{3,2,1,0:T(8,128)} fusion(f32[1,2,128,2048]{3,2,1,0:T(8,128)} %get-tuple-element.4, f32[2,2,128,2048]{3,2,1,0:T(8,128)S(1)} %copy-done, pred[]{:T(512)S(6)} %eq.3), kind=kLoop, calls=%fused_computation | loop fusion | flops 524288 | bytes 6291457 | tf_op jit(solution)/shard_map/jit(_where)/select_n | solution.py:437
  88.7 0.0 copy-done.1
  88.7 0.5 copy.9
Async XLA Ops:
  1.3 84.2 %copy-start = (f32[2,2,128,2048]{3,2,1,0:T(8,128)S(1)}, f32[2,2,128,2048]{3,2,1,0:T(8,128)}, u32[]{:S(2)}) copy-start(f32[2,2,128,2048]{3,2,1,0:T(8,128)} %fresh.1) | copy-start | bytes 12582916
  85.5 3.3 %copy-start.1 = (f32[1,128]{1,0:T(1,128)S(1)}, f32[1,128]{1,0:T(1,128)}, u32[]{:S(2)}) copy-start(f32[1,128]{1,0:T(1,128)} %get-tuple-element.9) | copy-start | bytes 1540
where the time goes:
time: 89.4 us; the launch traced here: 89.3 us
  Pallas kernels  84.2 us (94%)
  other arithmetic  3.27 us (4%)
  between operations  1.31 us (1%)
    pallas_call x1, Pallas kernels, body(): pl.pallas_call(kernel, name='relay', out_shape=(jax.ShapeDtypeStruct(stat...  84.2 us
    select_n x1, other arithmetic, body(): return (jnp.where(entered, fresh[1][None], out), image)  3.27 us

commit v1 on v0

--- a/solution.py
+++ b/solution.py
@@ -13,6 +13,7 @@
 ND = 16
 NS = 16
 NP = NS // 2
+CHUNKS = 4
 
 
 def dot(a, b):
@@ -37,8 +38,8 @@
 def kernel(
     freq, band, state, fresh, operators, out, image,
     x, ops, a_hi, a_lo, b0_hi, b0_lo, b1_hi, b1_lo, wr_hi, wr_lo, ws0, ws1,
-    send1, recv1, send2, recv2, obuf, tiles, y, i0, i1, r0, r1,
-    in_sem, out_sem, s1_sem, r1_sem, s2_sem, r2_sem, sb_sem, rb_sem, sy_sem, ry_sem, si_sem, ri_sem,
+    send1, recv1, send2, recv2, tiles, y, i0, i1, i2, r0, r1,
+    in_sem, s1_sem, r1_sem, s2_sem, r2_sem, sb_sem, rb_sem, sy_sem, ry_sem, si_sem, ri_sem,
 ):
     d, me = lax.axis_index("depth"), lax.axis_index("slab")
     c = lax.rem(d, 2)
@@ -49,6 +50,8 @@
     there1 = wrap(d + 2 * c)
     there2 = wrap(d + 2 * (1 - c))
     last = d == ND - 1
+    ends = d == ND - 2
+    first = d == 0
     relayed = d == 1
     at = lambda depth, slab: {"depth": depth, "slab": slab}
 
@@ -57,9 +60,9 @@
         pltpu.make_async_copy(state.at[0, :, :, q * 512 : q * 512 + 512], x.at[:, :, q * 512 : q * 512 + 512], in_sem.at[1 + q])
         for q in range(4)
     ]
-    ops_in.start()
     for copy in x_in:
         copy.start()
+    ops_in.start()
 
     barrier = pltpu.get_barrier_semaphore()
     signal = lambda depth, slab: pl.semaphore_signal(barrier, inc=1, device_id=at(depth, slab), device_id_type=MESH)
@@ -115,9 +118,6 @@
         ref[0 : 2 * W, 0:W] = jnp.zeros((2 * W, W), BF16)
         ref[NS * 2 * W :, W : 2 * W] = jnp.zeros((2 * W, W), BF16)
 
-    ops_in.wait()
-    build_r(operator(d, 0, 3))
-
     def put_a(block, re, im):
         for offset, value in ((0, re), (1, im)):
             hi, lo = split(value)
@@ -131,6 +131,9 @@
         @pl.loop(4 * q, 4 * q + 4)
         def _(b):
             put_a(b, x[0, :, lanes(b)], x[1, :, lanes(b)])
+
+    ops_in.wait()
+    build_r(operator(d, 0, 3))
 
     def along_receivers(p):
         first, second = lanes(4 * p, 6), lanes(4 * p + 2, 6)
@@ -157,6 +160,8 @@
     for copy in band_copies:
         copy.start()
 
+    part_rows = lambda h: pl.ds(pl.multiple_of(h * (W // CHUNKS), W // CHUNKS), W // CHUNKS)
+
     def copy1(t):
         return pltpu.make_async_remote_copy(
             src_ref=send1.at[t], dst_ref=recv1.at[me], send_sem=s1_sem.at[t], recv_sem=r1_sem.at[me],
@@ -169,21 +174,25 @@
             device_id=at(there1, j), device_id_type=MESH,
         )
 
-    def start1(t):
+    def start1(t, h):
         stays = (c == 0) & (t == me)
+        rows, to = part_rows(h), recv1.at[me, :, part_rows(h)]
 
         @pl.when(stays)
         def _():
-            pltpu.make_async_copy(send1.at[t], recv1.at[me], r1_sem.at[me]).start()
+            pltpu.make_async_copy(send1.at[t, :, rows], to, r1_sem.at[me]).start()
 
         @pl.when(jnp.logical_not(stays | last))
         def _():
-            copy1(t).start()
+            pltpu.make_async_remote_copy(
+                src_ref=send1.at[t, :, rows], dst_ref=to, send_sem=s1_sem.at[t], recv_sem=r1_sem.at[me],
+                device_id=at(there1, t), device_id_type=MESH,
+            ).start()
 
         @pl.when(last)
         def _():
             pltpu.make_async_remote_copy(
-                src_ref=fresh.at[0, :, :, lanes(t)], dst_ref=recv1.at[me], send_sem=s1_sem.at[t], recv_sem=r1_sem.at[me],
+                src_ref=fresh.at[0, :, rows, lanes(t)], dst_ref=to, send_sem=s1_sem.at[t], recv_sem=r1_sem.at[me],
                 device_id=at(there1, t), device_id_type=MESH,
             ).start()
 
@@ -199,16 +208,20 @@
             device_id=at(there2, j), device_id_type=MESH,
         )
 
-    def start2(t):
+    def start2(t, h):
         stays = (c == 1) & (t == me)
+        rows, to = part_rows(h), recv2.at[me, :, part_rows(h)]
 
         @pl.when(stays)
         def _():
-            pltpu.make_async_copy(send2.at[t], recv2.at[me], r2_sem.at[me]).start()
-
-        @pl.when(jnp.logical_not(stays))
-        def _():
-            copy2(t).start()
+            pltpu.make_async_copy(send2.at[t, :, rows], to, r2_sem.at[me]).start()
+
+        @pl.when(jnp.logical_not(stays | ends))
+        def _():
+            pltpu.make_async_remote_copy(
+                src_ref=send2.at[t, :, rows], dst_ref=to, send_sem=s2_sem.at[t], recv_sem=r2_sem.at[me],
+                device_id=at(there2, t), device_id_type=MESH,
+            ).start()
 
     @pl.loop(0, NP)
     def _(i):
@@ -217,20 +230,51 @@
         for n in range(2):
             for part in range(2):
                 send1[2 * p + n, part] = done[n * W : n * W + W, part * W : part * W + W]
-        start1(2 * p)
-        start1(2 * p + 1)
-
-    y_right = pltpu.make_async_remote_copy(
-        src_ref=send1.at[jnp.minimum(me + 1, NS - 1)], dst_ref=y.at[0], send_sem=sy_sem.at[0], recv_sem=ry_sem.at[0],
-        device_id=at(d, jnp.minimum(me + 1, NS - 1)), device_id_type=MESH,
-    )
-    y_left = pltpu.make_async_remote_copy(
-        src_ref=send1.at[jnp.maximum(me - 1, 0)], dst_ref=y.at[1], send_sem=sy_sem.at[1], recv_sem=ry_sem.at[1],
-        device_id=at(d, jnp.maximum(me - 1, 0)), device_id_type=MESH,
-    )
-    has_right, has_left = last & (me < NS - 1), last & (me > 0)
-    pl.when(has_right)(y_right.start)
-    pl.when(has_left)(y_left.start)
+        start1(2 * p, 0)
+        start1(2 * p + 1, 0)
+
+    @pl.loop(NP, CHUNKS * NP)
+    def _(i):
+        p = lax.rem(pair - i + CHUNKS * NP, NP)
+        start1(2 * p, i // NP)
+        start1(2 * p + 1, i // NP)
+
+    up, down = jnp.minimum(me + 1, NS - 1), jnp.maximum(me - 1, 0)
+    has_up, has_down = me < NS - 1, me > 0
+
+    def edges(send):
+        return [
+            pltpu.make_async_remote_copy(
+                src_ref=send.at[to], dst_ref=y.at[n], send_sem=sy_sem.at[n], recv_sem=ry_sem.at[n],
+                device_id=at(d, to), device_id_type=MESH,
+            )
+            for n, to in ((0, up), (1, down))
+        ]
+
+    def send_edges(when, send):
+        to_up, to_down = edges(send)
+        pl.when(when & has_up)(to_up.start)
+        pl.when(when & has_down)(to_down.start)
+
+    def take_edges(send, part, turn):
+        to_up, to_down = edges(send)
+        pl.when(has_down)(to_up.wait_recv)
+        pl.when(has_up)(to_down.wait_recv)
+        for n, has in ((0, has_down), (1, has_up)):
+
+            @pl.when(jnp.logical_not(has))
+            def _():
+                y[n] = jnp.zeros((2, W, W), F32)
+
+        total = jnp.zeros((1, W), F32)
+        for block, value in ((0, y[0]), (1, send[me]), (2, y[1])):
+            re, im = turn(value[0]), turn(value[1])
+            total += jnp.sum(re * part(0, block) - im * part(1, block), axis=0, keepdims=True)
+        pl.when(has_up)(to_up.wait_send)
+        pl.when(has_down)(to_down.wait_send)
+        return jnp.broadcast_to(total, (8, W))
+
+    send_edges(last, send1)
 
     for copy in band_copies:
         copy.wait_recv()
@@ -286,8 +330,14 @@
             done = along_shots(p, ws1, b1_hi, b1_lo)
             for n in range(2):
                 send2[2 * p + n] = done[:, n * W : n * W + W].reshape(2, W, W)
-            start2(2 * p)
-            start2(2 * p + 1)
+            start2(2 * p, 0)
+            start2(2 * p + 1, 0)
+
+    @pl.loop(NP, CHUNKS * NP)
+    def _(i):
+        p = lax.rem(pair + 2 + i, NP)
+        start2(2 * p, i // NP)
+        start2(2 * p + 1, i // NP)
 
     image0 = pltpu.make_async_remote_copy(
         src_ref=i0, dst_ref=r0, send_sem=si_sem.at[0], recv_sem=ri_sem.at[0], device_id=at(before, me), device_id_type=MESH
@@ -295,65 +345,54 @@
     sends_image0 = (c == 1) & jnp.logical_not(relayed)
     pl.when(sends_image0)(image0.start)
 
+    send_edges(ends, send2)
+
     @pl.when(last)
     def _():
-        @pl.when(me > 0)
-        def _():
-            y_right.wait_recv()
-
-        @pl.when(me < NS - 1)
-        def _():
-            y_left.wait_recv()
-
-        @pl.when(me == 0)
-        def _():
-            y[0] = jnp.zeros((2, W, W), F32)
-
-        @pl.when(me == NS - 1)
-        def _():
-            y[1] = jnp.zeros((2, W, W), F32)
-
-        part = operator(d, 0, 3)
-        total = jnp.zeros((1, W), F32)
-        for block, value in ((0, y[0]), (1, send1[me]), (2, y[1])):
-            total += jnp.sum(value[0] * part(0, block) - value[1] * part(1, block), axis=0, keepdims=True)
-        r0[...] = jnp.broadcast_to(total, (8, W))
+        r0[...] = take_edges(send1, operator(d, 0, 3), lambda v: v)
 
     image1 = pltpu.make_async_remote_copy(
         src_ref=i1, dst_ref=r1, send_sem=si_sem.at[1], recv_sem=ri_sem.at[1], device_id=at(wrap(d - 1), me), device_id_type=MESH
     )
-
-    def out_copy(p):
-        return pltpu.make_async_copy(obuf.at[:, :, lanes(2 * p, 2)], out.at[0, :, :, lanes(2 * p, 2)], out_sem.at[p])
-
-    @pl.loop(0, NP + 2)
-    def _(i):
-        @pl.when(i < NP)
-        def _():
-            p = lax.rem(pair - 2 - i + 2 * NP, NP)
-            for n in range(2):
-                arrival2(2 * p + n).wait_recv()
-                put_a(2 * p + n, recv2[2 * p + n, 0], recv2[2 * p + n, 1])
-
-        @pl.when(i >= 2)
-        def _():
-            p = lax.rem(pair - 3 - (i - 2) + 2 * NP, NP)
-            done = along_receivers(p)
-            for part in range(2):
-                obuf[part, :, lanes(2 * p)] = done[:W, part * W : part * W + W]
-                obuf[part, :, lanes(2 * p + 1)] = done[W:, part * W : part * W + W]
-            out_copy(p).start()
-
-            @pl.when(p == pair)
-            def _():
-                square = jnp.where(odd == 0, done[:W, :W], done[W:, :W])
-                i1[...] = jnp.broadcast_to(diagonal(square), (8, W))
-                image1.start()
+    image2 = pltpu.make_async_remote_copy(
+        src_ref=i2, dst_ref=r1, send_sem=si_sem.at[2], recv_sem=ri_sem.at[1], device_id=at(wrap(d + 1), me), device_id_type=MESH
+    )
+
+    @pl.when(ends)
+    def _():
+        i2[...] = take_edges(send2, operator(wrap(d + 1), 1, 2), lambda v: v.T)
+        image2.start()
+
+    fresh_out = pltpu.make_async_copy(fresh.at[1], out.at[0], in_sem.at[5])
+    pl.when(first)(fresh_out.start)
+
+    @pl.when(jnp.logical_not(first))
+    def _():
+        @pl.loop(0, NP + 2)
+        def _(i):
+            @pl.when(i < NP)
+            def _():
+                p = lax.rem(pair - 2 - i + 2 * NP, NP)
+                for n in range(2):
+                    arrival2(2 * p + n).wait_recv()
+                    put_a(2 * p + n, recv2[2 * p + n, 0], recv2[2 * p + n, 1])
+
+            @pl.when(i >= 2)
+            def _():
+                p = lax.rem(pair - 3 - (i - 2) + 2 * NP, NP)
+                done = along_receivers(p)
+                for part in range(2):
+                    out[0, part, :, lanes(2 * p)] = done[:W, part * W : part * W + W]
+                    out[0, part, :, lanes(2 * p + 1)] = done[W:, part * W : part * W + W]
+
+                @pl.when(p == pair)
+                def _():
+                    square = jnp.where(odd == 0, done[:W, :W], done[W:, :W])
+                    i1[...] = jnp.broadcast_to(diagonal(square), (8, W))
+                    image1.start()
 
     for copy in band_copies:
         copy.wait_send()
-    pl.when(has_right)(y_right.wait_send)
-    pl.when(has_left)(y_left.wait_send)
 
     @pl.loop(0, NS)
     def _(t):
@@ -361,13 +400,15 @@
         def _():
             copy1(t).wait_send()
 
-        @pl.when(jnp.logical_not((c == 1) & (t == me)))
+        @pl.when(jnp.logical_not((c == 1) & (t == me) | ends))
         def _():
             copy2(t).wait_send()
 
     pl.when(sends_image0)(image0.wait_send)
-    image1.wait_send()
+    pl.when(jnp.logical_not(first))(image1.wait_send)
+    pl.when(ends)(image2.wait_send)
     image1.wait_recv()
+    pl.when(first)(fresh_out.wait)
     pl.when((c == 1) & jnp.logical_not(last))(image0.wait_recv)
 
     @pl.when(c == 0)
@@ -378,13 +419,9 @@
     def _():
         image[...] = r0[0:1, :] + r1[0:1, :]
 
-    @pl.loop(0, NP)
-    def _(p):
-        out_copy(p).wait()
-
 
 def body(state, fresh, operators, band, freq_sched):
-    any_space = pl.BlockSpec(memory_space=pl.ANY)
+    any_space = pl.BlockSpec(memory_space=pltpu.HBM)
     smem = pl.BlockSpec(memory_space=pltpu.SMEM)
     dma, vmem = pltpu.SemaphoreType.DMA, pltpu.VMEM
     rows = state.shape[2]
@@ -393,7 +430,7 @@
         name="relay",
         out_shape=(jax.ShapeDtypeStruct(state.shape, F32), jax.ShapeDtypeStruct((1, rows), F32)),
         in_specs=[smem, smem, any_space, any_space, any_space],
-        out_specs=(any_space, pl.BlockSpec(memory_space=pltpu.VMEM)),
+        out_specs=(pl.BlockSpec(memory_space=pltpu.VMEM), pl.BlockSpec(memory_space=pltpu.VMEM)),
         scratch_shapes=[
             vmem(state.shape[1:], F32),
             vmem(operators.shape, F32),
@@ -411,15 +448,14 @@
             vmem((NS, 2, W, W), F32),
             vmem((NS, 2, W, W), F32),
             vmem((NS, 2, W, W), F32),
-            vmem(state.shape[1:], F32),
             vmem((4, 8, W), jnp.int32),
             vmem((2, 2, W, W), F32),
             vmem((8, W), F32),
             vmem((8, W), F32),
             vmem((8, W), F32),
             vmem((8, W), F32),
-            dma((5,)),
-            dma((NP,)),
+            vmem((8, W), F32),
+            dma((6,)),
             dma((NS,)),
             dma((NS,)),
             dma((NS,)),
@@ -428,13 +464,12 @@
             dma((3,)),
             dma((2,)),
             dma((2,)),
-            dma((2,)),
+            dma((3,)),
             dma((2,)),
         ],
-        compiler_params=pltpu.CompilerParams(collective_id=0, has_side_effects=True, vmem_limit_bytes=56 << 20),
-    )(freq_sched, band, state, fresh, operators)
-    entered = lax.axis_index("depth") == 0
-    return jnp.where(entered, fresh[1][None], out), image
+        compiler_params=pltpu.CompilerParams(collective_id=0, has_side_effects=True, vmem_limit_bytes=36 << 20),
+    )(freq_sched, band, *(pltpu.with_memory_space_constraint(v, pltpu.HBM) for v in (state, fresh, operators)))
+    return out, image
 
 
 def solution(mesh):

time: 89.4 us -> 74.9 us (0.84)
  the two profiles are of different devices: /device:TPU:137 before, /device:TPU:97 now
where the time goes in v1:
time: 74.9 us; the launch traced here: 74.8 us
  Pallas kernels  71 us (95%)
  local copies, waits for them, and re-layouts  2.48 us (3%)
  between operations  1.29 us (2%)
    pallas_call x1, Pallas kernels, body(): pl.pallas_call(kernel, name='relay', out_shape=(jax.ShapeDtypeStruct(stat...  71 us
    unnamed x4, local copies, waits for them, and re-layouts  2.48 us

profile of v1, /device:TPU:97, one launch (start us, length us, event | category | flops | bytes accessed | tf_op | source)
XLA Modules:
  0.0 74.8 jit_solution(11439487753214686494)
XLA Ops:
  1.3 0.0 copy-start
  1.3 0.6 copy-done
  1.9 71.0 %relay.1 = (f32[1,2,128,2048]{3,2,1,0:T(8,128)S(1)}, f32[1,128]{1,0:T(1,128)S(1)}) custom-call(s32[18]{0:T(128)S(1)} %copy-done, s32[1]{0:T(128)S(6)} %copy.9.band, f32[1,2,128,2048]{3,2,1,0:T(8,128)} %state.1, f32[2,2,128,2048]{3,2,1,0:T(8,128)} %fresh.1, f32[4,2,2,384,128]{4,3,2,1,0:T(8,128)} %operators.1), custom_call_target="tpu_custom_call" | custom-call | tf_op jit(solution)/shard_map/relay/pallas_call | solution.py:428
  72.9 1.3 %copy.10 = f32[1,2,128,2048]{3,2,1,0:T(8,128)} copy(f32[1,2,128,2048]{3,2,1,0:T(8,128)S(1)} %get-tuple-element.4) | data formatting | bytes 4194304
  74.3 0.5 copy.11
Async XLA Ops:
  1.3 0.7 copy-start

commit v2 on v1

--- a/solution.py
+++ b/solution.py
@@ -125,12 +125,16 @@
             a_hi[:, where] = hi
             a_lo[:, where] = lo
 
-    for q in range(4):
-        x_in[q].wait()
-
-        @pl.loop(4 * q, 4 * q + 4)
-        def _(b):
+    def put_pair(p):
+        for b in (2 * p, 2 * p + 1):
             put_a(b, x[0, :, lanes(b)], x[1, :, lanes(b)])
+
+    for copy in x_in:
+        copy.wait()
+
+    @pl.loop(0, 2)
+    def _(i):
+        put_pair(lax.rem(pair + i, NP))
 
     ops_in.wait()
     build_r(operator(d, 0, 3))
@@ -139,13 +143,12 @@
         first, second = lanes(4 * p, 6), lanes(4 * p + 2, 6)
         hi = jnp.concatenate([a_hi[:, first], a_hi[:, second]], axis=0)
         lo = jnp.concatenate([a_lo[:, first], a_lo[:, second]], axis=0)
-        both = dot(jnp.concatenate([hi, lo], axis=0), wr_hi[...])
-        return both[: 2 * W] + both[2 * W :] + dot(hi, wr_lo[...])
+        return dot(jnp.concatenate([hi, hi, lo], axis=1), jnp.concatenate([wr_hi[...], wr_lo[...], wr_hi[...]], axis=0))
 
     def along_shots(p, ws, b_hi, b_lo):
         rows = pl.ds(pl.multiple_of(p * 4 * W, 4 * W), 6 * W)
-        both = dot(ws[...], b_hi[rows, :])
-        return both[: 2 * W] + both[2 * W :] + dot(ws[: 2 * W, :], b_lo[rows, :])
+        hi, lo = ws[: 2 * W, :], ws[2 * W :, :]
+        return dot(jnp.concatenate([hi, lo, hi], axis=1), jnp.concatenate([b_hi[rows, :], b_hi[rows, :], b_lo[rows, :]], axis=0))
 
     pl.semaphore_wait(barrier, 2 * NS - 1 + 3)
 
@@ -226,6 +229,11 @@
     @pl.loop(0, NP)
     def _(i):
         p = lax.rem(pair - i + NP, NP)
+
+        @pl.when(i < NP - 2)
+        def _():
+            put_pair(lax.rem(pair - i - 1 + NP, NP))
+
         done = along_receivers(p)
         for n in range(2):
             for part in range(2):
@@ -292,6 +300,8 @@
         b_lo[down, 0:W] = lo
         b_lo[here, W : 2 * W] = lo
 
+    two = c == 1
+
     @pl.loop(0, NP + 4)
     def _(i):
         @pl.when(i < NP)
@@ -333,11 +343,18 @@
             start2(2 * p, 0)
             start2(2 * p + 1, 0)
 
+            @pl.when(two)
+            def _():
+                start2(2 * p, 1)
+                start2(2 * p + 1, 1)
+
     @pl.loop(NP, CHUNKS * NP)
     def _(i):
-        p = lax.rem(pair + 2 + i, NP)
-        start2(2 * p, i // NP)
-        start2(2 * p + 1, i // NP)
+        @pl.when((i >= 2 * NP) | jnp.logical_not(two))
+        def _():
+            p = lax.rem(pair - 1 + i, NP)
+            start2(2 * p, i // NP)
+            start2(2 * p + 1, i // NP)
 
     image0 = pltpu.make_async_remote_copy(
         src_ref=i0, dst_ref=r0, send_sem=si_sem.at[0], recv_sem=ri_sem.at[0], device_id=at(before, me), device_id_type=MESH
@@ -372,14 +389,14 @@
         def _(i):
             @pl.when(i < NP)
             def _():
-                p = lax.rem(pair - 2 - i + 2 * NP, NP)
+                p = lax.rem(pair + 1 - i + NP, NP)
                 for n in range(2):
                     arrival2(2 * p + n).wait_recv()
                     put_a(2 * p + n, recv2[2 * p + n, 0], recv2[2 * p + n, 1])
 
             @pl.when(i >= 2)
             def _():
-                p = lax.rem(pair - 3 - (i - 2) + 2 * NP, NP)
+                p = lax.rem(pair - (i - 2) + NP, NP)
                 done = along_receivers(p)
                 for part in range(2):
                     out[0, part, :, lanes(2 * p)] = done[:W, part * W : part * W + W]

time: 74.9 us -> 72.6 us (0.969)
  the two profiles are of different devices: /device:TPU:97 before, /device:TPU:128 now
where the time goes in v2:
time: 72.6 us; the launch traced here: 72.5 us
  Pallas kernels  68.7 us (95%)
  local copies, waits for them, and re-layouts  2.48 us (3%)
  between operations  1.29 us (2%)
    pallas_call x1, Pallas kernels, body(): pl.pallas_call(kernel, name='relay', out_shape=(jax.ShapeDtypeStruct(stat...  68.7 us
    unnamed x4, local copies, waits for them, and re-layouts  2.48 us

profile of v2, /device:TPU:128, one launch (start us, length us, event | category | flops | bytes accessed | tf_op | source)
XLA Modules:
  0.0 72.5 jit_solution(16405642794820363555)
XLA Ops:
  1.3 0.0 copy-start
  1.3 0.6 copy-done
  1.9 68.7 %relay.1 = (f32[1,2,128,2048]{3,2,1,0:T(8,128)S(1)}, f32[1,128]{1,0:T(1,128)S(1)}) custom-call(s32[18]{0:T(128)S(1)} %copy-done, s32[1]{0:T(128)S(6)} %copy.9.band, f32[1,2,128,2048]{3,2,1,0:T(8,128)} %state.1, f32[2,2,128,2048]{3,2,1,0:T(8,128)} %fresh.1, f32[4,2,2,384,128]{4,3,2,1,0:T(8,128)} %operators.1), custom_call_target="tpu_custom_call" | custom-call | tf_op jit(solution)/shard_map/relay/pallas_call | solution.py:445
  70.7 1.3 %copy.10 = f32[1,2,128,2048]{3,2,1,0:T(8,128)} copy(f32[1,2,128,2048]{3,2,1,0:T(8,128)S(1)} %get-tuple-element.4) | data formatting | bytes 4194304
  72.0 0.5 copy.11
Async XLA Ops:
  1.3 0.7 copy-start

commit v3 on v2

--- a/solution.py
+++ b/solution.py
@@ -300,7 +300,7 @@
         b_lo[down, 0:W] = lo
         b_lo[here, W : 2 * W] = lo
 
-    two = c == 1
+    two = (d != 7) & (d != 9)
 
     @pl.loop(0, NP + 4)
     def _(i):

time: 72.6 us -> 72.5 us (level)
  the two profiles are of different devices: /device:TPU:128 before, /device:TPU:137 now
where the time goes in v3:
time: 72.5 us; the launch traced here: 71.6 us
  Pallas kernels  67.8 us (94%)
  local copies, waits for them, and re-layouts  2.48 us (3%)
  between operations  1.29 us (2%)
    pallas_call x1, Pallas kernels, body(): pl.pallas_call(kernel, name='relay', out_shape=(jax.ShapeDtypeStruct(stat...  67.8 us
    unnamed x4, local copies, waits for them, and re-layouts  2.48 us

profile of v3, /device:TPU:137, one launch (start us, length us, event | category | flops | bytes accessed | tf_op | source)
XLA Modules:
  0.0 71.6 jit_solution(8380197560046783266)
XLA Ops:
  1.3 0.0 copy-start
  1.3 0.6 copy-done
  1.9 67.8 %relay.1 = (f32[1,2,128,2048]{3,2,1,0:T(8,128)S(1)}, f32[1,128]{1,0:T(1,128)S(1)}) custom-call(s32[18]{0:T(128)S(1)} %copy-done, s32[1]{0:T(128)S(6)} %copy.9.band, f32[1,2,128,2048]{3,2,1,0:T(8,128)} %state.1, f32[2,2,128,2048]{3,2,1,0:T(8,128)} %fresh.1, f32[4,2,2,384,128]{4,3,2,1,0:T(8,128)} %operators.1), custom_call_target="tpu_custom_call" | custom-call | tf_op jit(solution)/shard_map/relay/pallas_call | solution.py:445
  69.8 1.3 %copy.10 = f32[1,2,128,2048]{3,2,1,0:T(8,128)} copy(f32[1,2,128,2048]{3,2,1,0:T(8,128)S(1)} %get-tuple-element.4) | data formatting | bytes 4194304
  71.1 0.5 copy.11
Async XLA Ops:
  1.3 0.7 copy-start
